TPU v7x, 32 devices: a whole 2x2x4 slice. The times are simulated.
32 devices in a mesh: row: 16 (over z, y, x), rep: 2 (over core).
Axes of the slice: x: 2, y: 2, z: 4, core: 2. Of those that a mesh axis runs over, the one named last changes fastest.
Arguments:
- node_feats: bfloat16 [4096, 256], P(('row', 'rep')), may hold values from -6 to 6
- edge_feats: bfloat16 [32768, 256], P(('row', 'rep')), may hold values from -6 to 6
- senders: int32 [32768], P(('row', 'rep')), may hold values from 0 to 4095, as said below
- receivers: int32 [32768], P(('row', 'rep')), may hold values from 0 to 4095, as said below
- edge_count: int32 [32], P(('row', 'rep')), may hold values from 512 to 1024, as said below
- w_edge_in: bfloat16 [768, 256], replicated, may hold values from -0.21875 to 0.21875
- w_edge_out: bfloat16 [256, 256], replicated, may hold values from -0.375 to 0.375
- gain_edge: float32 [256], replicated, may hold values from 0.5 to 2
- w_node_in: bfloat16 [512, 256], replicated, may hold values from -0.25 to 0.25
- w_node_out: bfloat16 [256, 256], replicated, may hold values from -0.375 to 0.375
- gain_node: float32 [256], replicated, may hold values from 0.5 to 2
- d_nodes_out: bfloat16 [4096, 256], P(('row', 'rep')), may hold values from -6 to 6
- d_edges_out: bfloat16 [32768, 256], P(('row', 'rep')), may hold values from -6 to 6
Outputs:
- nodes_out: bfloat16 [4096, 256], P(('row', 'rep'))
- edges_out: bfloat16 [32768, 256], P(('row', 'rep'))
- d_nodes: bfloat16 [4096, 256], P(('row', 'rep'))
- d_edges: bfloat16 [32768, 256], P(('row', 'rep'))
- d_w_edge_in: bfloat16 [768, 256], replicated
- d_w_edge_out: bfloat16 [256, 256], replicated
- d_gain_edge: float32 [256], replicated
- d_w_node_in: bfloat16 [512, 256], replicated
- d_w_node_out: bfloat16 [256, 256], replicated
- d_gain_node: float32 [256], replicated
Inputs may be any that keep to these rules, and one draw needn't show every extreme that they name: `receivers`: edge i's receiver lies in nodes g * 256 to (g + 1) * 256 - 1 with g = i // 2048. `senders`: an edge's sender differs from its receiver by at most 128; in every aligned block of 1024 edge slots some edge reaches 128. The first edge_count[k] slots of the k-th aligned block of 1024 slots are live; some block is full.
All inputs are finite; a program needn't handle non-finite values.
Results may differ from a plain program's by a relative error of at most 0.013.
Values may be sent and summed in bfloat16 or wider, within the bound.
A program may use at most 64 MiB of HBM per device.

v0:
```python
import jax
import jax.numpy as jnp
from jax import lax
from jax.sharding import PartitionSpec as P


def padded(x, sides, width):
    for axis, dim in sides:
        devices, length = (lax.axis_size(axis), x.shape[dim])
        up = [(i, (i + 1) % devices) for i in range(devices - 1)]
        down = [(j, i) for i, j in up]
        last = lax.slice_in_dim(x, length - width, length, axis=dim)
        first = lax.slice_in_dim(x, 0, width, axis=dim)
        before = lax.ppermute(last, axis, up)
        after = lax.ppermute(first, axis, down)
        x = jnp.concatenate([before, x, after], axis=dim)
    return x


def from_behind(value, axis, steps):
    count = lax.axis_size(axis)
    first, last = (max(0, -steps), min(count, count - steps))
    return lax.ppermute(value, axis, [(source, source + steps) for source in range(first, last)])


def silu_slope(pre):
    sigmoid = jax.nn.sigmoid(pre)
    return sigmoid * (1.0 + pre * (1.0 - sigmoid))


def layer_norm(values):
    centred = values - jnp.mean(values, axis=-1, keepdims=True)
    inv_scale = lax.rsqrt(jnp.mean(centred * centred, axis=-1, keepdims=True) + 1e-05)
    return (centred * inv_scale, inv_scale)


def norm_back(upstream, normed, inv_scale):
    return inv_scale * (
        upstream
        - jnp.mean(upstream, axis=-1, keepdims=True)
        - normed * jnp.mean(upstream * normed, axis=-1, keepdims=True)
    )


def contract_rows(left, right):
    return lax.dot_general(
        left, right, (((0,), (0,)), ((), ())), preferred_element_type=jnp.float32
    )


def times_transpose(left, right):
    return lax.dot_general(
        left, right, (((1,), (1,)), ((), ())), preferred_element_type=jnp.float32
    )


def local(
    node_feats,
    edge_feats,
    senders,
    receivers,
    edge_count,
    w_edge_in,
    w_edge_out,
    gain_edge,
    w_node_in,
    w_node_out,
    gain_node,
    d_nodes_out,
    d_edges_out,
):
    width = node_feats.shape[1]
    edge_rows = edge_feats.shape[0]
    grouped = lax.all_gather(node_feats, "rep", axis=0, tiled=True)
    group_rows = grouped.shape[0]
    rim_rows = group_rows // 2
    extended = padded(grouped, (("row", 0),), rim_rows)
    group_start = lax.axis_index("row") * group_rows
    recv_local = receivers - group_start
    send_local = senders - group_start + rim_rows
    slots = jnp.arange(edge_rows, dtype=jnp.int32)
    live_mask = (slots < edge_count[0]).astype(jnp.float32)[:, None]
    edge_input = jnp.concatenate(
        [edge_feats, jnp.take(extended, send_local, axis=0), jnp.take(grouped, recv_local, axis=0)],
        axis=1,
    )
    edge_pre = jnp.dot(edge_input, w_edge_in, preferred_element_type=jnp.float32)
    edge_act = jax.nn.silu(edge_pre).astype(jnp.bfloat16)
    edge_mix = jnp.dot(edge_act, w_edge_out, preferred_element_type=jnp.float32)
    edge_norm, edge_scale = layer_norm(edge_mix)
    message = live_mask * edge_norm * gain_edge
    edges_out = (edge_feats.astype(jnp.float32) + message).astype(jnp.bfloat16)
    message_b = message.astype(jnp.bfloat16)
    recv_table = (
        lax.broadcasted_iota(jnp.int32, (group_rows, edge_rows), 0) == recv_local[None, :]
    ).astype(jnp.bfloat16)
    partial_sums = jnp.dot(recv_table, message_b, preferred_element_type=jnp.float32)
    aggregate = lax.psum_scatter(partial_sums, "rep", scatter_dimension=0, tiled=True)
    node_input = jnp.concatenate([node_feats, aggregate.astype(jnp.bfloat16)], axis=1)
    node_pre = jnp.dot(node_input, w_node_in, preferred_element_type=jnp.float32)
    node_act = jax.nn.silu(node_pre).astype(jnp.bfloat16)
    node_mix = jnp.dot(node_act, w_node_out, preferred_element_type=jnp.float32)
    node_norm, node_scale = layer_norm(node_mix)
    nodes_out = (node_feats.astype(jnp.float32) + node_norm * gain_node).astype(jnp.bfloat16)
    grad_nodes = d_nodes_out.astype(jnp.float32)
    d_gain_node = jnp.sum(grad_nodes * node_norm, axis=0)
    d_node_mix = norm_back(grad_nodes * gain_node, node_norm, node_scale).astype(jnp.bfloat16)
    d_w_node_out = contract_rows(node_act, d_node_mix)
    d_node_pre = (times_transpose(d_node_mix, w_node_out) * silu_slope(node_pre)).astype(
        jnp.bfloat16
    )
    d_w_node_in = contract_rows(node_input, d_node_pre)
    d_node_input = times_transpose(d_node_pre, w_node_in)
    d_aggregate = d_node_input[:, width:].astype(jnp.bfloat16)
    d_direct = grad_nodes + d_node_input[:, :width]
    group_grad = lax.all_gather(d_aggregate, "rep", axis=0, tiled=True)
    d_message = live_mask * (
        d_edges_out.astype(jnp.float32)
        + jnp.take(group_grad, recv_local, axis=0).astype(jnp.float32)
    )
    d_gain_edge = jnp.sum(d_message * edge_norm, axis=0)
    d_edge_mix = norm_back(d_message * gain_edge, edge_norm, edge_scale).astype(jnp.bfloat16)
    d_w_edge_out = contract_rows(edge_act, d_edge_mix)
    d_edge_pre = (times_transpose(d_edge_mix, w_edge_out) * silu_slope(edge_pre)).astype(
        jnp.bfloat16
    )
    d_w_edge_in = contract_rows(edge_input, d_edge_pre)
    d_edge_input = times_transpose(d_edge_pre, w_edge_in)
    d_edges = (d_edges_out.astype(jnp.float32) + d_edge_input[:, :width]).astype(jnp.bfloat16)
    d_sender = d_edge_input[:, width : 2 * width].astype(jnp.bfloat16)
    d_receiver = d_edge_input[:, 2 * width :].astype(jnp.bfloat16)
    send_table = (
        lax.broadcasted_iota(jnp.int32, (group_rows + 2 * rim_rows, edge_rows), 0)
        == send_local[None, :]
    ).astype(jnp.bfloat16)
    send_sums = jnp.dot(send_table, d_sender, preferred_element_type=jnp.float32)
    recv_sums = jnp.dot(recv_table, d_receiver, preferred_element_type=jnp.float32)
    from_next = from_behind(send_sums[:rim_rows].astype(jnp.bfloat16), "row", -1).astype(
        jnp.float32
    )
    from_prev = from_behind(
        send_sums[group_rows + rim_rows :].astype(jnp.bfloat16), "row", 1
    ).astype(jnp.float32)
    inner = send_sums[rim_rows : rim_rows + group_rows]
    inner = jnp.concatenate([inner[:rim_rows] + from_prev, inner[rim_rows:] + from_next], axis=0)
    edge_terms = lax.psum_scatter(
        inner.astype(jnp.bfloat16), "rep", scatter_dimension=0, tiled=True
    ).astype(jnp.float32) + lax.psum_scatter(
        recv_sums.astype(jnp.bfloat16), "rep", scatter_dimension=0, tiled=True
    ).astype(
        jnp.float32
    )
    d_nodes = (d_direct + edge_terms).astype(jnp.bfloat16)
    summed = lax.psum(
        (d_w_edge_in, d_w_edge_out, d_gain_edge, d_w_node_in, d_w_node_out, d_gain_node),
        ("row", "rep"),
    )
    return (
        nodes_out,
        edges_out,
        d_nodes,
        d_edges,
        summed[0].astype(jnp.bfloat16),
        summed[1].astype(jnp.bfloat16),
        summed[2],
        summed[3].astype(jnp.bfloat16),
        summed[4].astype(jnp.bfloat16),
        summed[5],
    )


def solution(mesh):
    return jax.shard_map(
        local,
        mesh=mesh,
        in_specs=(
            P(("row", "rep"), None),
            P(("row", "rep"), None),
            P(("row", "rep")),
            P(("row", "rep")),
            P(("row", "rep")),
            P(),
            P(),
            P(),
            P(),
            P(),
            P(),
            P(("row", "rep"), None),
            P(("row", "rep"), None),
        ),
        out_specs=(
            P(("row", "rep"), None),
            P(("row", "rep"), None),
            P(("row", "rep"), None),
            P(("row", "rep"), None),
            P(),
            P(),
            P(),
            P(),
            P(),
            P(),
        ),
        check_vma=False,
    )
```

profile of v0, /device:TPU:0, one launch (start us, length us, event | category | flops | bytes accessed | tf_op | source)
XLA Modules:
  0.0 151.7 jit_solution(1003866890800980398)
XLA Ops:
  7.2 2.4 %all_gather.6 = bf16[256,256]{1,0:T(8,128)(2,1)S(1)} all-gather(bf16[128,256]{1,0:T(8,128)(2,1)} %param.15), channel_id=1, replica_groups=mesh['row'=16,'rep'=2] {'rep'}, dimensions={0}, use_global_device_ids=true | all-gather | bytes 196608 | tf_op jit(solution)/shard_map/all_gather | solution.py:74
  9.6 4.7 %collective-permute-start = (bf16[128,256]{1,0:T(8,128)(2,1)S(1)}, bf16[128,256]{1,0:T(8,128)(2,1)S(1)}, u32[]{:S(2)}, u32[]{:S(2)}) collective-permute-start(bf16[128,256]{1,0:T(8,128)(2,1)S(1)} %get-tuple-element.42), channel_id=1, source_target_pairs={{0,2},{2,4},{4,6},{6,8},{8,10},{10,12},{12,14},{14,16},{16,18},{18... | collective-permute-start | bytes 196616 | tf_op jit(solution)/shard_map/ppermute | solution.py:14
  14.4 1.3 collective-permute-start.1
  16.4 1.3 subtract_add_fusion
  18.3 0.7 compare_and_fusion
  19.0 3.9 %gather_fusion.1 = bf16[1024,256]{1,0:T(8,128)(2,1)S(1)} fusion(bf16[256,256]{1,0:T(8,128)(2,1)S(1)} %all_gather.6, s32[1024]{0:T(1024)S(1)} %fusion.36), kind=kCustom, calls=%fused_computation.clone | custom fusion | bytes 1052672 | tf_op jit(solution)/shard_map/jit(_take)/gather | solution.py:84
  23.3 3.9 %gather_fusion = bf16[1024,256]{1,0:T(8,128)(2,1)S(1)} fusion(bf16[512,256]{1,0:T(8,128)(2,1)S(1)} %pad_maximum_fusion.3, s32[1024]{0:T(1024)S(1)} %get-tuple-element.45), kind=kCustom, calls=%fused_computation.2 | custom fusion | bytes 1052672 | tf_op jit(solution)/shard_map/jit(_take)/gather | solution.py:84
  27.5 1.6 %multiply_convert_fusion.1 = (bf16[1024,256]{1,0:T(8,128)(2,1)S(1)}, f32[1024,256]{1,0:T(8,128)}) fusion(bf16[768,256]{1,0:T(8,128)(2,1)S(1)} %copy-done, bf16[1024,256]{1,0:T(8,128)(2,1)S(1)} %broadcast_select_fusion, bf16[1024,256]{1,0:T(8,128)(2,1)S(1)} %broadcast_select_fusion.1, bf16[1024,256]{1,0:T(8,128)(2,1)S(1)} %copy-done.17), kind=kOutput, calls=%fused_computation.22 | convolution fusion | flops 408682496 | bytes 3538944 | tf_op jit(solution)/shard_map/dot_general | solution.py:87
  29.8 1.2 fusion.6
  31.0 1.0 copy.23
  32.3 9.0 %reduce-scatter.4.cloned.1.call-done = f32[128,256]{1,0:T(8,128)} async-done(((f32[256,256]{1,0:T(8,128)}), f32[128,256]{1,0:T(8,128)}) %reduce-scatter.4.cloned.1.call-update) | async-done | bytes 131088 | tf_op jit(solution)/shard_map/reduce_scatter | solution.py:98
  41.3 0.9 convert_element_type.98
  42.4 1.2 fusion.48
  43.8 1.3 fusion.30
  45.4 1.0 fusion.41
  47.3 1.9 %all_gather.7 = bf16[256,256]{1,0:T(8,128)(2,1)S(1)} all-gather(bf16[128,256]{1,0:T(8,128)(2,1)S(1)} %slice.81), channel_id=1, replica_groups=mesh['row'=16,'rep'=2] {'rep'}, dimensions={0}, use_global_device_ids=true | all-gather | bytes 196608 | tf_op jit(solution)/shard_map/all_gather | solution.py:116
  49.2 3.9 %gather_fusion.2 = bf16[1024,256]{1,0:T(8,128)(2,1)S(1)} fusion(bf16[256,256]{1,0:T(8,128)(2,1)S(1)} %all_gather.7, s32[1024]{0:T(1024)S(1)} %fusion.36), kind=kCustom, calls=%fused_computation.1.clone | custom fusion | bytes 1052672 | tf_op jit(solution)/shard_map/jit(_take)/gather | solution.py:119
  53.4 1.9 %multiply_reduce_fusion = (f32[256]{0:T(256)}, f32[1024]{0:T(1024)S(1)}, f32[1024]{0:T(1024)S(1)}) fusion(bf16[1024,256]{0,1:T(8,128)(2,1)S(1)} %copy.24, f32[1024,256]{0,1:T(8,128)S(1)} %get-tuple-element.49, f32[1024]{0:T(1024)S(1)} %add_rsqrt_fusion, f32[1024]{0:T(1024)S(1)} %broadcast_multiply_fusion.2, f32[1024]{0:T(1024)S(1)} %fusion.35, ...), kind=kLoop, calls=%fused_computation.15 | loop fusion | flops 3405568 | bytes 2120704 | tf_op jit(solution)/shard_map/reduce_sum | solution.py:121
  55.3 1.5 multiply_convert_fusion
  56.8 1.1 fusion.52
  59.2 1.5 fusion.10
  60.7 1.8 %fusion.49 = (bf16[1024,768]{1,0:T(8,128)(2,1)}, f32[1024,768]{1,0:T(8,128)S(1)}) fusion(bf16[1024,256]{1,0:T(8,128)(2,1)S(1)} %fusion.1, bf16[768,256]{1,0:T(8,128)(2,1)S(1)} %copy-done), kind=kOutput, calls=%fused_computation.99 | convolution fusion | flops 403439616 | bytes 5636096 | tf_op jit(solution)/shard_map/dot_general | solution.py:52
  63.6 2.0 %convolution_convert_fusion = bf16[256,256]{1,0:T(8,128)(2,1)} fusion(bf16[1024,768]{1,0:T(8,128)(2,1)} %get-tuple-element.52, s32[1024]{0:T(1024)S(1)} %copy-done.27), kind=kOutput, calls=%fused_computation.10 | convolution fusion | flops 134545408 | bytes 659456 | tf_op jit(solution)/shard_map/dot_general | solution.py:137
  65.6 2.4 %fusion.50 = (bf16[512,256]{1,0:T(8,128)(2,1)S(1)}, f32[512,256]{1,0:T(8,128)}) fusion(bf16[1024,768]{1,0:T(8,128)(2,1)} %get-tuple-element.52, s32[1024]{0:T(1024)S(1)} %copy-done.31), kind=kOutput, calls=%fused_computation.100 | convolution fusion | flops 269090816 | bytes 1314816 | tf_op jit(solution)/shard_map/dot_general | solution.py:136
  68.0 3.6 %collective-permute-start.2 = (bf16[128,256]{1,0:T(8,128)(2,1)S(1)}, bf16[128,256]{1,0:T(8,128)(2,1)S(1)}, u32[]{:S(2)}, u32[]{:S(2)}) collective-permute-start(bf16[128,256]{1,0:T(8,128)(2,1)S(1)} %get-tuple-element.39), channel_id=1, source_target_pairs={{0,2},{2,4},{4,6},{6,8},{8,10},{10,12},{12,14},{14,16},{16,18},{18... | collective-permute-start | bytes 196616 | tf_op jit(solution)/shard_map/ppermute | solution.py:23
  71.6 1.3 collective-permute-start.3
  73.2 1.0 copy.27
  74.2 1.0 copy.28
  75.3 2.4 %collective-permute-done.3 = bf16[128,256]{1,0:T(8,128)(2,1)S(1)} collective-permute-done((bf16[128,256]{1,0:T(8,128)(2,1)S(1)}, bf16[128,256]{1,0:T(8,128)(2,1)S(1)}, u32[]{:S(2)}, u32[]{:S(2)}) %collective-permute-start.3) | collective-permute-done | bytes 65568 | tf_op jit(solution)/shard_map/ppermute | solution.py:23
  77.7 1.0 fusion.32
  79.5 64.1 %all-reduce.2 = (bf16[768,256]{1,0:T(8,128)(2,1)}, bf16[256,256]{1,0:T(8,128)(2,1)}, f32[256]{0:T(256)}, bf16[512,256]{1,0:T(8,128)(2,1)}, bf16[256,256]{1,0:T(8,128)(2,1)}, /*index=5*/f32[256]{0:T(256)}) all-reduce(f32[768,256]{1,0:T(8,128)S(1)} %copy-done.9, ...), channel_id=1, replica_groups=mesh['row'=16,'rep'=2] {'row','rep'}, use_global_device_ids=true, to_apply=%region_11.13 | all-reduce | flops 459264 | bytes 2756608 | tf_op jit(solution)/shard_map/psum | solution.py:154
  143.6 1.5 %fusion.29 = bf16[128,256]{1,0:T(8,128)(2,1)} fusion(bf16[128,256]{1,0:T(8,128)(2,1)S(1)} %copy-done.21, f32[128,512]{1,0:T(8,128)S(1)} %copy-done.8, bf16[128,256]{1,0:T(8,128)(2,1)} %reduce-scatter.8.cloned.1.call-done, bf16[128,256]{1,0:T(8,128)(2,1)} %reduce-scatter.6.cloned.1.call-done), kind=kLoop, calls=%fused_computation.55 | loop fusion | flops 229376 | bytes 393216 | tf_op jit(solution)/shard_map/convert_element_type | solution.py:153
  (117 shorter events, 7.4 us)
Async XLA Ops:
  7.2 20.3 %copy-start = (bf16[768,256]{1,0:T(8,128)(2,1)S(1)}, bf16[768,256]{1,0:T(8,128)(2,1)}, u32[]{:S(2)}) copy-start(bf16[768,256]{1,0:T(8,128)(2,1)} %param.20) | copy-start | bytes 1179652
  7.2 34.1 %reduce-scatter.4.cloned.1.call-start = ((), (), s32[]{:S(2)}) async-start(), calls=%async_computation.3 | async-start | bytes 393216 | tf_op jit(solution)/shard_map/reduce_scatter | solution.py:98
  9.6 13.6 %collective-permute-start = (bf16[128,256]{1,0:T(8,128)(2,1)S(1)}, bf16[128,256]{1,0:T(8,128)(2,1)S(1)}, u32[]{:S(2)}, u32[]{:S(2)}) collective-permute-start(bf16[128,256]{1,0:T(8,128)(2,1)S(1)} %get-tuple-element.42), channel_id=1, source_target_pairs={{0,2},{2,4},{4,6},{6,8},{8,10},{10,12},{12,14},{14,16},{16,18},{18... | collective-permute-start | bytes 196616 | tf_op jit(solution)/shard_map/ppermute | solution.py:14
  14.4 8.9 %collective-permute-start.1 = (bf16[128,256]{1,0:T(8,128)(2,1)S(1)}, bf16[128,256]{1,0:T(8,128)(2,1)S(1)}, u32[]{:S(2)}, u32[]{:S(2)}) collective-permute-start(bf16[128,256]{1,0:T(8,128)(2,1)S(1)} %get-tuple-element.43), channel_id=1, source_target_pairs={{2,0},{4,2},{6,4},{8,6},{10,8},{12,10},{14,12},{16,14},{18,16},{20... | collective-permute-start | bytes 196616 | tf_op jit(solution)/shard_map/ppermute | solution.py:15
  19.0 4.0 %copy-start.28 = (pred[1024]{0:T(1024)(128)(4,1)}, pred[1024]{0:T(1024)(128)(4,1)S(1)}, u32[]{:S(2)}) copy-start(pred[1024]{0:T(1024)(128)(4,1)S(1)} %get-tuple-element.33) | copy-start | bytes 3076
  19.0 10.6 %copy-start.26 = (s32[1024]{0:T(1024)}, s32[1024]{0:T(1024)S(1)}, u32[]{:S(2)}) copy-start(s32[1024]{0:T(1024)S(1)} %get-tuple-element.34) | copy-start | bytes 12292
  23.2 4.2 %copy-start.12 = (bf16[1024,256]{1,0:T(8,128)(2,1)}, bf16[1024,256]{1,0:T(8,128)(2,1)S(1)}, u32[]{:S(2)}) copy-start(bf16[1024,256]{1,0:T(8,128)(2,1)S(1)} %broadcast_select_fusion) | copy-start | bytes 1572868
  23.3 4.2 %copy-start.17 = (bf16[1024,256]{1,0:T(8,128)(2,1)S(1)}, bf16[1024,256]{1,0:T(8,128)(2,1)}, u32[]{:S(2)}) copy-start(bf16[1024,256]{1,0:T(8,128)(2,1)} %param.16) | copy-start | bytes 1572868
  30.9 11.2 %copy-start.3 = (bf16[512,256]{1,0:T(8,128)(2,1)S(1)}, bf16[512,256]{1,0:T(8,128)(2,1)}, u32[]{:S(2)}) copy-start(bf16[512,256]{1,0:T(8,128)(2,1)} %param.23) | copy-start | bytes 786436
  30.9 11.3 %copy-start.5 = (bf16[128,256]{1,0:T(8,128)(2,1)S(1)}, bf16[128,256]{1,0:T(8,128)(2,1)}, u32[]{:S(2)}) copy-start(bf16[128,256]{1,0:T(8,128)(2,1)} %param.15) | copy-start | bytes 196612
  31.0 12.8 %copy-start.20 = (bf16[128,256]{1,0:T(8,128)(2,1)S(1)}, bf16[128,256]{1,0:T(8,128)(2,1)}, u32[]{:S(2)}) copy-start(bf16[128,256]{1,0:T(8,128)(2,1)} %param.26) | copy-start | bytes 196612
  31.0 12.8 %copy-start.35 = (f32[256]{0:T(256)S(1)}, f32[256]{0:T(256)}, u32[]{:S(2)}) copy-start(f32[256]{0:T(256)} %param.25) | copy-start | bytes 3076
  31.0 112.6 %reduce-scatter.8.cloned.1.call-start = ((), (), s32[]{:S(2)}) async-start(), calls=%async_computation.5 | async-start | bytes 196608 | tf_op jit(solution)/shard_map/reduce_scatter | solution.py:148
  32.2 12.9 %copy-start.36 = (bf16[256,256]{1,0:T(8,128)(2,1)S(1)}, bf16[256,256]{1,0:T(8,128)(2,1)}, u32[]{:S(2)}) copy-start(bf16[256,256]{1,0:T(8,128)(2,1)} %param.24) | copy-start | bytes 393220
  42.2 3.2 %copy-start.10 = (bf16[128,256]{1,0:T(8,128)(2,1)}, bf16[128,256]{1,0:T(8,128)(2,1)S(1)}, u32[]{:S(2)}) copy-start(bf16[128,256]{1,0:T(8,128)(2,1)S(1)} %convert_element_type.98) | copy-start | bytes 196612
  45.4 3.8 %copy-start.22 = (bf16[128,256]{1,0:T(8,128)(2,1)}, bf16[128,256]{1,0:T(8,128)(2,1)S(1)}, u32[]{:S(2)}) copy-start(bf16[128,256]{1,0:T(8,128)(2,1)S(1)} %fusion.2) | copy-start | bytes 196612
  55.3 2.5 %copy-start.25 = (bf16[256,256]{1,0:T(8,128)(2,1)S(1)}, bf16[256,256]{1,0:T(8,128)(2,1)}, u32[]{:S(2)}) copy-start(bf16[256,256]{1,0:T(8,128)(2,1)} %param.21) | copy-start | bytes 393220
  62.9 2.7 %copy-start.31 = (s32[1024]{0:T(1024)S(1)}, s32[1024]{0:T(1024)}, u32[]{:S(2)}) copy-start(s32[1024]{0:T(1024)} %get-tuple-element.44) | copy-start | bytes 12292
  63.6 9.3 %copy-start.6 = (bf16[128,256]{1,0:T(8,128)(2,1)S(1)}, bf16[128,256]{1,0:T(8,128)(2,1)}, u32[]{:S(2)}) copy-start(bf16[128,256]{1,0:T(8,128)(2,1)} %param.15) | copy-start | bytes 196612
  63.6 9.3 %copy-start.11 = (bf16[128,256]{1,0:T(8,128)(2,1)S(1)}, bf16[128,256]{1,0:T(8,128)(2,1)}, u32[]{:S(2)}) copy-start(bf16[128,256]{1,0:T(8,128)(2,1)} %copy-done.10) | copy-start | bytes 196612
  63.6 9.3 %copy-start.23 = (bf16[128,256]{1,0:T(8,128)(2,1)S(1)}, bf16[128,256]{1,0:T(8,128)(2,1)}, u32[]{:S(2)}) copy-start(bf16[128,256]{1,0:T(8,128)(2,1)} %copy-done.22) | copy-start | bytes 196612
  65.6 7.5 %copy-start.2 = (bf16[1024,256]{0,1:T(8,128)(2,1)S(1)}, bf16[1024,256]{0,1:T(8,128)(2,1)}, u32[]{:S(2)}) copy-start(bf16[1024,256]{0,1:T(8,128)(2,1)} %get-tuple-element.36) | copy-start | bytes 1572868
  68.0 7.3 %collective-permute-start.2 = (bf16[128,256]{1,0:T(8,128)(2,1)S(1)}, bf16[128,256]{1,0:T(8,128)(2,1)S(1)}, u32[]{:S(2)}, u32[]{:S(2)}) collective-permute-start(bf16[128,256]{1,0:T(8,128)(2,1)S(1)} %get-tuple-element.39), channel_id=1, source_target_pairs={{0,2},{2,4},{4,6},{6,8},{8,10},{10,12},{12,14},{14,16},{16,18},{18... | collective-permute-start | bytes 196616 | tf_op jit(solution)/shard_map/ppermute | solution.py:23
  71.6 6.2 %collective-permute-start.3 = (bf16[128,256]{1,0:T(8,128)(2,1)S(1)}, bf16[128,256]{1,0:T(8,128)(2,1)S(1)}, u32[]{:S(2)}, u32[]{:S(2)}) collective-permute-start(bf16[128,256]{1,0:T(8,128)(2,1)S(1)} %get-tuple-element.40), channel_id=1, source_target_pairs={{2,0},{4,2},{6,4},{8,6},{10,8},{12,10},{14,12},{16,14},{18,16},{20... | collective-permute-start | bytes 196616 | tf_op jit(solution)/shard_map/ppermute | solution.py:23
  73.2 6.2 %copy-start.4 = (f32[256,256]{1,0:T(8,128)S(1)}, f32[256,256]{1,0:T(8,128)}, u32[]{:S(2)}) copy-start(f32[256,256]{1,0:T(8,128)} %fusion.52) | copy-start | bytes 786436
  73.2 6.2 %copy-start.9 = (f32[768,256]{1,0:T(8,128)S(1)}, f32[768,256]{1,0:T(8,128)}, u32[]{:S(2)}) copy-start(f32[768,256]{1,0:T(8,128)} %fusion.10) | copy-start | bytes 2359300
  73.2 6.2 %copy-start.19 = (f32[256,256]{1,0:T(8,128)S(1)}, f32[256,256]{1,0:T(8,128)}, u32[]{:S(2)}) copy-start(f32[256,256]{1,0:T(8,128)} %fusion.41) | copy-start | bytes 786436
  73.2 6.2 %copy-start.30 = (f32[256]{0:T(256)S(1)}, f32[256]{0:T(256)}, u32[]{:S(2)}) copy-start(f32[256]{0:T(256)} %get-tuple-element.21) | copy-start | bytes 3076
  73.2 6.2 %copy-start.32 = (f32[256]{0:T(256)S(1)}, f32[256]{0:T(256)}, u32[]{:S(2)}) copy-start(f32[256]{0:T(256)} %get-tuple-element.24) | copy-start | bytes 3076
  75.2 68.4 %copy-start.8 = (f32[128,512]{1,0:T(8,128)S(1)}, f32[128,512]{1,0:T(8,128)}, u32[]{:S(2)}) copy-start(f32[128,512]{1,0:T(8,128)} %copy-done.7) | copy-start | bytes 786436
  75.2 68.4 %copy-start.21 = (bf16[128,256]{1,0:T(8,128)(2,1)S(1)}, bf16[128,256]{1,0:T(8,128)(2,1)}, u32[]{:S(2)}) copy-start(bf16[128,256]{1,0:T(8,128)(2,1)} %param.26) | copy-start | bytes 196612
  75.2 68.4 %reduce-scatter.6.cloned.1.call-start = ((), (), s32[]{:S(2)}) async-start(), calls=%async_computation.4 | async-start | bytes 196608 | tf_op jit(solution)/shard_map/reduce_scatter | solution.py:146
  (13 other events, 19.7 us)
Sparse Core Ops, SparseCore 0:
  31.1 10.1 reduce-scatter.3
  75.4 9.6 reduce-scatter.7
  87.3 8.7 reduce-scatter.5
where the time goes:
time: 152 us
  blocking collectives  68.4 us (45%)
  local copies, waits for them, and re-layouts  18 us (12%)
  matrix products  15.5 us (10%)
  between operations  15 us (10%)
  other arithmetic  12.3 us (8%)
  waiting for transfers between devices  11.5 us (8%)
  starting transfers between devices  11 us (7%)
    psum x1, blocking collectives, local(): lax.psum((d_w_edge_in, d_w_edge_out, d_gain_edge, d_w_node_in, d_w_node_o...  64.1 us
    reduce_scatter x1, waiting for transfers between devices, local(): lax.psum_scatter(partial_sums, 'rep', scatter_dimension=0, tiled=True)  9 us
    unnamed x81, local copies, waits for them, and re-layouts  5.84 us
    ppermute x2, starting transfers between devices, from_behind(): lax.ppermute(value, axis, [(source, source + steps) for source in range(f...  4.84 us
    ppermute x1, starting transfers between devices, padded(): before = lax.ppermute(last, axis, up)  4.74 us
    gather x2, local copies, waits for them, and re-layouts, local(): jnp.take(group_grad, recv_local, axis=0).astype(jnp.float32)  4.14 us
    gather x1, local copies, waits for them, and re-layouts, local(): jnp.take(grouped, recv_local, axis=0)  3.94 us
    gather x1, local copies, waits for them, and re-layouts, local(): jnp.take(extended, send_local, axis=0)  3.94 us
  transfers between devices with their start and end apart: 7, of which 2 were waited for; matrix products, arithmetic and copies ran while one was open for 8% of the time, Pallas kernels for 0%

commit v1 on v0

--- a/solution.py
+++ b/solution.py
@@ -152,8 +152,10 @@
     )
     d_nodes = (d_direct + edge_terms).astype(jnp.bfloat16)
     summed = lax.psum(
-        (d_w_edge_in, d_w_edge_out, d_gain_edge, d_w_node_in, d_w_node_out, d_gain_node),
-        ("row", "rep"),
+        lax.psum(
+            (d_w_edge_in, d_w_edge_out, d_gain_edge, d_w_node_in, d_w_node_out, d_gain_node), "rep"
+        ),
+        "row",
     )
     return (
         nodes_out,

time: 152 us -> 221 us (1.45)
  blocking collectives: 68.4 us -> 103 us
  waiting for transfers between devices: 11.5 us -> 43.8 us
    psum x0 -> x1, blocking collectives: none -> 96.1 us  [local(): lax.psum(lax.psum((d_w_edge_in, d_w_edge_out, d_gain_edge, d_w_node_in, d...]
    psum x1, blocking collectives: 64.1 us -> 2.45 us  [local(): lax.psum((d_w_edge_in, d_w_edge_out, d_gain_edge, d_w_node_in, d_w_node_o...]
    psum x0 -> x1, waiting for transfers between devices: none -> 23.7 us  [local(): lax.psum((d_w_edge_in, d_w_edge_out, d_gain_edge, d_w_node_in, d_w_node_o...]
    reduce_scatter x1, waiting for transfers between devices: 0.01 us -> 8.02 us  [local(): lax.psum_scatter(inner.astype(jnp.bfloat16), 'rep', scatter_dimension=0,...]
    unnamed x81 -> x105, local copies, waits for them, and re-layouts: 5.84 us -> 6.76 us
  transfers between devices with their start and end apart: 7 -> 8, of which waited for: 2 -> 4; matrix products, arithmetic and copies ran while one was open for 8% -> 8% of each run, Pallas kernels for 0% -> 0%
where the time goes in v1:
time: 221 us
  blocking collectives  103 us (47%)
  waiting for transfers between devices  43.8 us (20%)
  local copies, waits for them, and re-layouts  20.1 us (9%)
  matrix products  15.2 us (7%)
  between operations  15.1 us (7%)
  other arithmetic  12.3 us (6%)
  starting transfers between devices  11.2 us (5%)
    psum x1, blocking collectives, local(): lax.psum(lax.psum((d_w_edge_in, d_w_edge_out, d_gain_edge, d_w_node_in, d...  96.1 us
    psum x1, waiting for transfers between devices, local(): lax.psum((d_w_edge_in, d_w_edge_out, d_gain_edge, d_w_node_in, d_w_node_o...  23.7 us
    reduce_scatter x1, waiting for transfers between devices, local(): lax.psum_scatter(partial_sums, 'rep', scatter_dimension=0, tiled=True)  8.99 us
    reduce_scatter x1, waiting for transfers between devices, local(): lax.psum_scatter(inner.astype(jnp.bfloat16), 'rep', scatter_dimension=0,...  8.02 us
    unnamed x105, local copies, waits for them, and re-layouts  6.76 us
    dot_general x4, matrix products, contract_rows(): lax.dot_general(left, right, (((0,), (0,)), ((), ())), preferred_element_...  5.26 us
    ppermute x2, starting transfers between devices, from_behind(): lax.ppermute(value, axis, [(source, source + steps) for source in range(f...  5 us
    ppermute x1, starting transfers between devices, padded(): before = lax.ppermute(last, axis, up)  4.74 us
  transfers between devices with their start and end apart: 8, of which 4 were waited for; matrix products, arithmetic and copies ran while one was open for 8% of the time, Pallas kernels for 0%

profile of v1, /device:TPU:0, one launch (start us, length us, event | category | flops | bytes accessed | tf_op | source)
XLA Modules:
  0.0 220.7 jit_solution(11098453348938133651)
XLA Ops:
  7.2 2.4 %all_gather.6 = bf16[256,256]{1,0:T(8,128)(2,1)S(1)} all-gather(bf16[128,256]{1,0:T(8,128)(2,1)} %param.15), channel_id=1, replica_groups=mesh['row'=16,'rep'=2] {'rep'}, dimensions={0}, use_global_device_ids=true | all-gather | bytes 196608 | tf_op jit(solution)/shard_map/all_gather | solution.py:74
  9.6 4.7 %collective-permute-start = (bf16[128,256]{1,0:T(8,128)(2,1)S(1)}, bf16[128,256]{1,0:T(8,128)(2,1)S(1)}, u32[]{:S(2)}, u32[]{:S(2)}) collective-permute-start(bf16[128,256]{1,0:T(8,128)(2,1)S(1)} %get-tuple-element.48), channel_id=1, source_target_pairs={{0,2},{2,4},{4,6},{6,8},{8,10},{10,12},{12,14},{14,16},{16,18},{18... | collective-permute-start | bytes 196616 | tf_op jit(solution)/shard_map/ppermute | solution.py:14
  14.4 1.3 collective-permute-start.1
  16.4 1.3 subtract_add_fusion
  19.6 3.9 %gather_fusion.1 = bf16[1024,256]{1,0:T(8,128)(2,1)S(1)} fusion(bf16[256,256]{1,0:T(8,128)(2,1)S(1)} %all_gather.6, s32[1024]{0:T(1024)S(1)} %fusion.36), kind=kCustom, calls=%fused_computation.clone | custom fusion | bytes 1052672 | tf_op jit(solution)/shard_map/jit(_take)/gather | solution.py:84
  23.9 3.9 %gather_fusion = bf16[1024,256]{1,0:T(8,128)(2,1)S(1)} fusion(bf16[512,256]{1,0:T(8,128)(2,1)S(1)} %pad_maximum_fusion.3, s32[1024]{0:T(1024)S(1)} %get-tuple-element.51), kind=kCustom, calls=%fused_computation.2 | custom fusion | bytes 1052672 | tf_op jit(solution)/shard_map/jit(_take)/gather | solution.py:84
  28.1 1.6 multiply_convert_fusion.1
  30.3 1.2 fusion.6
  31.6 1.0 copy.23
  32.8 9.0 %reduce-scatter.4.cloned.1.call-done = f32[128,256]{1,0:T(8,128)} async-done(((f32[256,256]{1,0:T(8,128)}), f32[128,256]{1,0:T(8,128)}) %reduce-scatter.4.cloned.1.call-update) | async-done | bytes 131088 | tf_op jit(solution)/shard_map/reduce_scatter | solution.py:98
  43.0 1.2 fusion.48
  44.4 2.1 fusion.30
  48.0 1.9 all_gather.7
  49.9 3.9 %gather_fusion.2 = bf16[1024,256]{1,0:T(8,128)(2,1)S(1)} fusion(bf16[256,256]{1,0:T(8,128)(2,1)S(1)} %all_gather.7, s32[1024]{0:T(1024)S(1)} %fusion.36), kind=kCustom, calls=%fused_computation.1.clone | custom fusion | bytes 1052672 | tf_op jit(solution)/shard_map/jit(_take)/gather | solution.py:119
  54.1 1.8 multiply_reduce_fusion
  58.6 1.5 fusion.10
  60.1 2.3 %fusion.49 = (bf16[1024,768]{1,0:T(8,128)(2,1)S(1)}, f32[1024,768]{1,0:T(8,128)}) fusion(bf16[1024,256]{1,0:T(8,128)(2,1)S(1)} %fusion.1, bf16[768,256]{1,0:T(8,128)(2,1)S(1)} %copy-done), kind=kOutput, calls=%fused_computation.99 | convolution fusion | flops 403439616 | bytes 5636096 | tf_op jit(solution)/shard_map/dot_general | solution.py:52
  63.4 1.3 fusion.50
  64.7 3.7 %collective-permute-start.2 = (bf16[128,256]{1,0:T(8,128)(2,1)S(1)}, bf16[128,256]{1,0:T(8,128)(2,1)S(1)}, u32[]{:S(2)}, u32[]{:S(2)}) collective-permute-start(bf16[128,256]{1,0:T(8,128)(2,1)S(1)} %get-tuple-element.45), channel_id=1, source_target_pairs={{0,2},{2,4},{4,6},{6,8},{8,10},{10,12},{12,14},{14,16},{16,18},{18... | collective-permute-start | bytes 196616 | tf_op jit(solution)/shard_map/ppermute | solution.py:23
  68.4 1.3 collective-permute-start.3
  69.8 1.6 fusion.41
  71.5 3.1 %collective-permute-done.3 = bf16[128,256]{1,0:T(8,128)(2,1)S(1)} collective-permute-done((bf16[128,256]{1,0:T(8,128)(2,1)S(1)}, bf16[128,256]{1,0:T(8,128)(2,1)S(1)}, u32[]{:S(2)}, u32[]{:S(2)}) %collective-permute-start.3) | collective-permute-done | bytes 65568 | tf_op jit(solution)/shard_map/ppermute | solution.py:23
  76.3 1.1 fusion.33
  77.4 1.0 fusion.52
  78.5 1.0 copy.27
  79.5 1.3 slice.68
  81.3 1.0 copy.28
  82.3 2.4 %all-reduce.1 = (f32[256]{0:T(256)S(1)}, f32[256]{0:T(256)S(1)}) all-reduce(f32[256]{0:T(256)S(1)} %copy-done.35, f32[256]{0:T(256)S(1)} %copy-done.37), channel_id=1, replica_groups=mesh['row'=16,'rep'=2] {'rep'}, use_global_device_ids=true, to_apply=%region_16.18 | all-reduce | flops 512 | bytes 4096 | tf_op jit(solution)/shard_map/psum | solution.py:155
  84.7 8.0 %reduce-scatter.6.cloned.1.call-done = bf16[128,256]{1,0:T(8,128)(2,1)} async-done(((bf16[256,256]{1,0:T(8,128)(2,1)}), bf16[128,256]{1,0:T(8,128)(2,1)}) %reduce-scatter.6.cloned.1.call-update) | async-done | bytes 65552 | tf_op jit(solution)/shard_map/reduce_scatter | solution.py:146
  92.8 1.5 fusion.29
  94.3 23.7 %all-reduce.6.cloned.1.call-done = (f32[768,256]{1,0:T(8,128)}, f32[256,256]{1,0:T(8,128)}, f32[512,256]{1,0:T(8,128)}, f32[256,256]{1,0:T(8,128)}) async-done(((f32[768,256]{1,0:T(8,128)}, f32[256,256]{1,0:T(8,128)}, f32[512,256]{1,0:T(8,128)}, f32[256,256]{1,0:T(8,128)}), (f32[768,256]{1,0:T(8,128)}, f32[256,256]{1,0:T(8,128)}, f32[512,256]{1,0:T(8,128)}, ...) | async-done | bytes 1835024 | tf_op jit(solution)/shard_map/psum | solution.py:155
  118.0 96.1 %all-reduce.7 = (bf16[768,256]{1,0:T(8,128)(2,1)}, bf16[256,256]{1,0:T(8,128)(2,1)}, f32[256]{0:T(256)}, bf16[512,256]{1,0:T(8,128)(2,1)}, bf16[256,256]{1,0:T(8,128)(2,1)}, /*index=5*/f32[256]{0:T(256)}) all-reduce(f32[768,256]{1,0:T(8,128)} %get-tuple-element.35, ...), channel_id=1, replica_groups=mesh['row'=16,'rep'=2] {'row'}, use_global_device_ids=true, to_apply=%region_12.14 | all-reduce | flops 459264 | bytes 2756608 | tf_op jit(solution)/shard_map/psum | solution.py:154
  (145 shorter events, 12.3 us)
Async XLA Ops:
  7.2 20.9 %copy-start = (bf16[768,256]{1,0:T(8,128)(2,1)S(1)}, bf16[768,256]{1,0:T(8,128)(2,1)}, u32[]{:S(2)}) copy-start(bf16[768,256]{1,0:T(8,128)(2,1)} %param.20) | copy-start | bytes 1179652
  7.2 34.6 %reduce-scatter.4.cloned.1.call-start = ((), (), s32[]{:S(2)}) async-start(), calls=%async_computation.3 | async-start | bytes 393216 | tf_op jit(solution)/shard_map/reduce_scatter | solution.py:98
  9.6 14.2 %collective-permute-start = (bf16[128,256]{1,0:T(8,128)(2,1)S(1)}, bf16[128,256]{1,0:T(8,128)(2,1)S(1)}, u32[]{:S(2)}, u32[]{:S(2)}) collective-permute-start(bf16[128,256]{1,0:T(8,128)(2,1)S(1)} %get-tuple-element.48), channel_id=1, source_target_pairs={{0,2},{2,4},{4,6},{6,8},{8,10},{10,12},{12,14},{14,16},{16,18},{18... | collective-permute-start | bytes 196616 | tf_op jit(solution)/shard_map/ppermute | solution.py:14
  14.4 9.4 %collective-permute-start.1 = (bf16[128,256]{1,0:T(8,128)(2,1)S(1)}, bf16[128,256]{1,0:T(8,128)(2,1)S(1)}, u32[]{:S(2)}, u32[]{:S(2)}) collective-permute-start(bf16[128,256]{1,0:T(8,128)(2,1)S(1)} %get-tuple-element.49), channel_id=1, source_target_pairs={{2,0},{4,2},{6,4},{8,6},{10,8},{12,10},{14,12},{16,14},{18,16},{20... | collective-permute-start | bytes 196616 | tf_op jit(solution)/shard_map/ppermute | solution.py:15
  19.0 4.5 %copy-start.33 = (pred[1024]{0:T(1024)(128)(4,1)}, pred[1024]{0:T(1024)(128)(4,1)S(1)}, u32[]{:S(2)}) copy-start(pred[1024]{0:T(1024)(128)(4,1)S(1)} %get-tuple-element.39) | copy-start | bytes 3076
  23.8 4.2 %copy-start.11 = (bf16[1024,256]{1,0:T(8,128)(2,1)}, bf16[1024,256]{1,0:T(8,128)(2,1)S(1)}, u32[]{:S(2)}) copy-start(bf16[1024,256]{1,0:T(8,128)(2,1)S(1)} %broadcast_select_fusion) | copy-start | bytes 1572868
  23.8 4.2 %copy-start.16 = (bf16[1024,256]{1,0:T(8,128)(2,1)S(1)}, bf16[1024,256]{1,0:T(8,128)(2,1)}, u32[]{:S(2)}) copy-start(bf16[1024,256]{1,0:T(8,128)(2,1)} %param.16) | copy-start | bytes 1572868
  31.5 11.2 %copy-start.4 = (bf16[512,256]{1,0:T(8,128)(2,1)S(1)}, bf16[512,256]{1,0:T(8,128)(2,1)}, u32[]{:S(2)}) copy-start(bf16[512,256]{1,0:T(8,128)(2,1)} %param.23) | copy-start | bytes 786436
  31.5 11.3 %copy-start.5 = (bf16[128,256]{1,0:T(8,128)(2,1)S(1)}, bf16[128,256]{1,0:T(8,128)(2,1)}, u32[]{:S(2)}) copy-start(bf16[128,256]{1,0:T(8,128)(2,1)} %param.15) | copy-start | bytes 196612
  31.5 53.2 %reduce-scatter.8.cloned.1.call-start = ((), (), s32[]{:S(2)}) async-start(), calls=%async_computation.5 | async-start | bytes 196608 | tf_op jit(solution)/shard_map/reduce_scatter | solution.py:148
  32.8 14.3 %copy-start.21 = (bf16[128,256]{1,0:T(8,128)(2,1)S(1)}, bf16[128,256]{1,0:T(8,128)(2,1)}, u32[]{:S(2)}) copy-start(bf16[128,256]{1,0:T(8,128)(2,1)} %param.26) | copy-start | bytes 196612
  32.8 14.3 %copy-start.42 = (f32[256]{0:T(256)S(1)}, f32[256]{0:T(256)}, u32[]{:S(2)}) copy-start(f32[256]{0:T(256)} %param.25) | copy-start | bytes 3076
  32.8 14.3 %copy-start.48 = (bf16[256,256]{1,0:T(8,128)(2,1)S(1)}, bf16[256,256]{1,0:T(8,128)(2,1)}, u32[]{:S(2)}) copy-start(bf16[256,256]{1,0:T(8,128)(2,1)} %param.24) | copy-start | bytes 393220
  42.8 3.8 %copy-start.9 = (bf16[128,256]{1,0:T(8,128)(2,1)}, bf16[128,256]{1,0:T(8,128)(2,1)S(1)}, u32[]{:S(2)}) copy-start(bf16[128,256]{1,0:T(8,128)(2,1)S(1)} %convert_element_type.98) | copy-start | bytes 196612
  43.0 4.7 %copy-start.26 = (f32[128,256]{1,0:T(8,128)}, f32[128,256]{1,0:T(8,128)S(1)}, u32[]{:S(2)}) copy-start(f32[128,256]{1,0:T(8,128)S(1)} %fusion.34) | copy-start | bytes 393220
  44.2 3.5 %copy-start.40 = (f32[128]{0:T(128)}, f32[128]{0:T(128)S(1)}, u32[]{:S(2)}) copy-start(f32[128]{0:T(128)S(1)} %broadcast_multiply_fusion.5) | copy-start | bytes 1540
  62.4 7.3 %copy-start.41 = (f32[128]{0:T(128)S(1)}, f32[128]{0:T(128)}, u32[]{:S(2)}) copy-start(f32[128]{0:T(128)} %copy-done.40) | copy-start | bytes 1540
  62.4 7.3 %copy-start.43 = (f32[256]{0:T(256)S(1)}, f32[256]{0:T(256)}, u32[]{:S(2)}) copy-start(f32[256]{0:T(256)} %param.25) | copy-start | bytes 3076
  62.4 7.3 %copy-start.45 = (f32[128]{0:T(128)S(1)}, f32[128]{0:T(128)}, u32[]{:S(2)}) copy-start(f32[128]{0:T(128)} %copy-done.44) | copy-start | bytes 1540
  63.4 6.3 %copy-start.20 = (f32[128,256]{1,0:T(8,128)S(1)}, f32[128,256]{1,0:T(8,128)}, u32[]{:S(2)}) copy-start(f32[128,256]{1,0:T(8,128)} %copy-done.19) | copy-start | bytes 393220
  63.4 6.3 %copy-start.22 = (bf16[128,256]{1,0:T(8,128)(2,1)S(1)}, bf16[128,256]{1,0:T(8,128)(2,1)}, u32[]{:S(2)}) copy-start(bf16[128,256]{1,0:T(8,128)(2,1)} %param.26) | copy-start | bytes 196612
  63.4 6.4 %copy-start.27 = (f32[128,256]{1,0:T(8,128)S(1)}, f32[128,256]{1,0:T(8,128)}, u32[]{:S(2)}) copy-start(f32[128,256]{1,0:T(8,128)} %copy-done.26) | copy-start | bytes 393220
  64.6 11.6 %copy-start.6 = (bf16[128,256]{1,0:T(8,128)(2,1)S(1)}, bf16[128,256]{1,0:T(8,128)(2,1)}, u32[]{:S(2)}) copy-start(bf16[128,256]{1,0:T(8,128)(2,1)} %param.15) | copy-start | bytes 196612
  64.7 11.6 %copy-start.10 = (bf16[128,256]{1,0:T(8,128)(2,1)S(1)}, bf16[128,256]{1,0:T(8,128)(2,1)}, u32[]{:S(2)}) copy-start(bf16[128,256]{1,0:T(8,128)(2,1)} %copy-done.9) | copy-start | bytes 196612
  64.7 11.7 %copy-start.25 = (bf16[128,256]{1,0:T(8,128)(2,1)S(1)}, bf16[128,256]{1,0:T(8,128)(2,1)}, u32[]{:S(2)}) copy-start(bf16[128,256]{1,0:T(8,128)(2,1)} %copy-done.24) | copy-start | bytes 196612
  64.7 12.7 %copy-start.2 = (bf16[1024,256]{0,1:T(8,128)(2,1)S(1)}, bf16[1024,256]{0,1:T(8,128)(2,1)}, u32[]{:S(2)}) copy-start(bf16[1024,256]{0,1:T(8,128)(2,1)} %copy-done.1) | copy-start | bytes 1572868
  64.7 6.8 %collective-permute-start.2 = (bf16[128,256]{1,0:T(8,128)(2,1)S(1)}, bf16[128,256]{1,0:T(8,128)(2,1)S(1)}, u32[]{:S(2)}, u32[]{:S(2)}) collective-permute-start(bf16[128,256]{1,0:T(8,128)(2,1)S(1)} %get-tuple-element.45), channel_id=1, source_target_pairs={{0,2},{2,4},{4,6},{6,8},{8,10},{10,12},{12,14},{14,16},{16,18},{18... | collective-permute-start | bytes 196616 | tf_op jit(solution)/shard_map/ppermute | solution.py:23
  68.4 6.2 %collective-permute-start.3 = (bf16[128,256]{1,0:T(8,128)(2,1)S(1)}, bf16[128,256]{1,0:T(8,128)(2,1)S(1)}, u32[]{:S(2)}, u32[]{:S(2)}) collective-permute-start(bf16[128,256]{1,0:T(8,128)(2,1)S(1)} %get-tuple-element.46), channel_id=1, source_target_pairs={{2,0},{4,2},{6,4},{8,6},{10,8},{12,10},{14,12},{16,14},{18,16},{20... | collective-permute-start | bytes 196616 | tf_op jit(solution)/shard_map/ppermute | solution.py:23
  71.4 21.4 %reduce-scatter.6.cloned.1.call-start = ((), (), s32[]{:S(2)}) async-start(), calls=%async_computation.4 | async-start | bytes 196608 | tf_op jit(solution)/shard_map/reduce_scatter | solution.py:146
  76.2 41.8 %all-reduce.6.cloned.1.call-start = ((), (), s32[]{:S(2)}) async-start(), calls=%async_computation.6 | async-start | bytes 3670016 | tf_op jit(solution)/shard_map/psum | solution.py:155
  81.1 11.7 %copy-start.8 = (f32[128,512]{1,0:T(8,128)S(1)}, f32[128,512]{1,0:T(8,128)}, u32[]{:S(2)}) copy-start(f32[128,512]{1,0:T(8,128)} %copy-done.7) | copy-start | bytes 786436
  81.1 11.6 %copy-start.23 = (bf16[128,256]{1,0:T(8,128)(2,1)S(1)}, bf16[128,256]{1,0:T(8,128)(2,1)}, u32[]{:S(2)}) copy-start(bf16[128,256]{1,0:T(8,128)(2,1)} %param.26) | copy-start | bytes 196612
  (26 other events, 39.5 us)
Sparse Core Ops, SparseCore 0:
  31.6 10.1 reduce-scatter.3
  71.5 9.6 reduce-scatter.7
  84.0 8.6 reduce-scatter.5
  95.8 22.1 all-reduce.5
